TPU v7x, 256 devices: a whole 4x4x8 slice. The times are simulated.
256 devices in a mesh: dp: 4 (over x), seq: 16 (over z, core), tensor: 4 (over y).
Axes of the slice: x: 4, y: 4, z: 8, core: 2. Of those that a mesh axis runs over, the one named last changes fastest.
Arguments:
- feature_in: bfloat16 [16, 2048, 512], P('dp', 'seq', 'tensor'), may hold values from -6 to 6
- conv_weight: bfloat16 [2, 512, 512], P(None, 'tensor'), may hold values from -0.1875 to 0.1875
- proj_weight: bfloat16 [512, 1920], P(None, 'tensor'), may hold values from -0.25 to 0.25
- mask_embed: bfloat16 [1920], P('tensor'), may hold values from -5 to 5
- pos_weight: bfloat16 [128, 16, 120, 120], P(('dp', 'seq'), 'tensor'), may hold values from -0.046875 to 0.046875
- final_weight: bfloat16 [1920, 1024], P('tensor'), may hold values from -0.125 to 0.125
- codebook: bfloat16 [2, 320, 512], replicated, may hold values from -6 to 6
- quant_weight: bfloat16 [1024, 1024], replicated, may hold values from -0.1875 to 0.1875
- mask_starts: int32 [16, 66], P('dp'), may hold values from 0 to 1014
- code_choice: int32 [16, 1024, 2], P(('dp', 'tensor'), 'seq'), may hold values from 0 to 319
- negative_ids: int32 [16, 1024, 100], P(('dp', 'tensor'), 'seq'), may hold values from 0 to 1023, as said below
Outputs:
- frame_loss: float32 [16, 1024], P(('dp', 'tensor'), 'seq')
Inputs may be any that keep to these rules, and one draw needn't show every extreme that they name: `negative_ids`: each entry names a frame of the same utterance other than the frame itself.
All inputs are finite; a program needn't handle non-finite values.
Results may differ from a plain program's by a relative error of at most 0.00065.
Values may be sent and summed in bfloat16 or wider, within the bound.
A program may use at most 128 MiB of HBM per device.

v0:
```python
import jax
import jax.numpy as jnp
from jax import lax
from jax.sharding import PartitionSpec as P

KERNEL = 128
MASK_LEN = 10
ln_eps = 1e-05
norm_eps = 1e-06
logit_temp = 0.1


def extended(block, sides, width):
    for axis, dim in sides:
        count = lax.axis_size(axis)
        forward = [(i, i + 1) for i in range(count - 1)]
        backward = [(target, source) for source, target in forward]
        low = lax.ppermute(
            lax.slice_in_dim(block, block.shape[dim] - width, None, axis=dim), axis, forward
        )
        high = lax.ppermute(lax.slice_in_dim(block, 0, width, axis=dim), axis, backward)
        block = jnp.concatenate([low, block, high], axis=dim)
    return block


def make_targets(code_block, codebook, quant_weight):
    entries = codebook.shape[1]
    choices_row = jnp.arange(entries, dtype=jnp.int32)
    pieces = []
    for qgroup in range(codebook.shape[0]):
        onehot = (code_block[..., qgroup, None] == choices_row).astype(jnp.bfloat16)
        pieces.append(
            jnp.dot(onehot, codebook[qgroup], preferred_element_type=jnp.float32).astype(
                jnp.bfloat16
            )
        )
    codevec = jnp.concatenate(pieces, axis=-1)
    return jnp.dot(codevec, quant_weight, preferred_element_type=jnp.float32).astype(jnp.bfloat16)


def utterance_loss(context, own_targets, all_targets, neg_ids, is_masked):
    scores = jnp.einsum("fc,nc->fn", context, all_targets, preferred_element_type=jnp.float32)
    ctx_norm = jnp.einsum("fc,fc->f", context, context, preferred_element_type=jnp.float32)
    own_norm = jnp.einsum("fc,fc->f", own_targets, own_targets, preferred_element_type=jnp.float32)
    tgt_norm = jnp.einsum("nc,nc->n", all_targets, all_targets, preferred_element_type=jnp.float32)
    pos_dot = jnp.einsum("fc,fc->f", context, own_targets, preferred_element_type=jnp.float32)
    neg_dot = jnp.take_along_axis(scores, neg_ids, axis=1)
    neg_norm = tgt_norm[neg_ids]
    positive = pos_dot * lax.rsqrt((ctx_norm + norm_eps) * (own_norm + norm_eps)) / logit_temp
    negative = (
        neg_dot * lax.rsqrt((ctx_norm[:, None] + norm_eps) * (neg_norm + norm_eps)) / logit_temp
    )
    frame_loss = jnp.log(jnp.exp(positive) + jnp.sum(jnp.exp(negative), axis=-1)) - positive
    return jnp.where(is_masked, frame_loss, jnp.zeros_like(frame_loss))


def tap_sum(windows, running, tap_block, frames):
    count = tap_block.shape[0]
    joined_taps = max((d for d in range(1, 17) if count % d == 0))
    group_count, inner, outer = (tap_block.shape[1], tap_block.shape[2], tap_block.shape[3])

    def add_block(step, partial_value):
        base = step * joined_taps
        slabs = [
            lax.dynamic_slice_in_dim(windows, base + offset, frames, 1)
            for offset in range(joined_taps)
        ]
        joined = jnp.concatenate(slabs, axis=-1)
        taps = lax.dynamic_slice_in_dim(tap_block, base, joined_taps, 0)
        taps = jnp.transpose(taps, (1, 0, 2, 3)).reshape(group_count, joined_taps * inner, outer)
        return partial_value + jnp.einsum(
            "ufgi,gio->ufgo", joined, taps, preferred_element_type=jnp.float32
        )

    return lax.fori_loop(0, count // joined_taps, add_block, running)


def on_device(
    feature_in,
    conv_weight,
    proj_weight,
    mask_embed,
    pos_weight,
    final_weight,
    codebook,
    quant_weight,
    mask_starts,
    code_choice,
    negative_ids,
):
    utt_count, sample_rows, channels = feature_in.shape
    frames = sample_rows // 2
    frame_pairs = feature_in.reshape(utt_count, frames, 2 * channels)
    conv_term = jnp.dot(
        frame_pairs,
        conv_weight.reshape(2 * channels, conv_weight.shape[2]),
        preferred_element_type=jnp.float32,
    )
    summed = lax.psum(conv_term, "tensor")
    row_mean = jnp.mean(summed, axis=-1, keepdims=True)
    row_square = jnp.mean(summed * summed, axis=-1, keepdims=True)
    normed = (summed - row_mean) * lax.rsqrt(row_square - row_mean * row_mean + ln_eps)
    features = jax.nn.gelu(normed, approximate=False).astype(jnp.bfloat16)
    projected = jnp.dot(features, proj_weight, preferred_element_type=jnp.float32).astype(
        jnp.bfloat16
    )
    positions = (lax.axis_index("seq") * frames + jnp.arange(frames, dtype=jnp.int32))[
        None, :, None
    ]
    starts = mask_starts[:, None, :]
    masked = jnp.any((positions >= starts) & (positions < starts + MASK_LEN), axis=-1)
    hidden = jnp.where(masked[..., None], mask_embed[None, None, :], projected)
    padded = extended(hidden, (("seq", 1),), KERNEL // 2)
    group_count = pos_weight.shape[1]
    inner = pos_weight.shape[2]
    outer = pos_weight.shape[3]
    windows = padded.reshape(utt_count, padded.shape[1], group_count, inner)
    initial = jnp.zeros((utt_count, frames, group_count, outer), jnp.float32)
    conv_out = tap_sum(
        windows, initial, lax.all_gather(pos_weight, ("dp", "seq"), axis=0, tiled=True), frames
    )
    conv_out = conv_out.reshape(utt_count, frames, group_count * outer)
    mixed = (hidden.astype(jnp.float32) + jax.nn.gelu(conv_out, approximate=False)).astype(
        jnp.bfloat16
    )
    utt_rows = utt_count // lax.axis_size("tensor")
    context = lax.psum_scatter(
        jnp.dot(mixed, final_weight, preferred_element_type=jnp.float32),
        "tensor",
        scatter_dimension=0,
        tiled=True,
    ).astype(jnp.bfloat16)
    own_targets = make_targets(code_choice, codebook, quant_weight)
    all_targets = lax.all_gather(own_targets, "seq", axis=1, tiled=True)
    is_masked = lax.dynamic_slice_in_dim(masked, lax.axis_index("tensor") * utt_rows, utt_rows, 0)
    return jax.vmap(utterance_loss)(context, own_targets, all_targets, negative_ids, is_masked)


def solution(mesh):
    return jax.shard_map(
        on_device,
        mesh=mesh,
        in_specs=(
            P("dp", "seq", "tensor"),
            P(None, "tensor", None),
            P(None, "tensor"),
            P("tensor"),
            P(("dp", "seq"), "tensor", None, None),
            P("tensor", None),
            P(),
            P(),
            P("dp", None),
            P(("dp", "tensor"), "seq", None),
            P(("dp", "tensor"), "seq", None),
        ),
        out_specs=P(("dp", "tensor"), "seq"),
        check_vma=False,
    )
```

profile of v0, /device:TPU:1, one launch (start us, length us, event | category | flops | bytes accessed | tf_op | source)
XLA Modules:
  0.0 506.4 jit_solution(2708013920155017598)
XLA Ops:
  12.7 48.5 %all-reduce.2.cloned.1.call-done = f32[4,64,512]{2,1,0:T(8,128)} async-done(((f32[4,64,512]{2,1,0:T(8,128)}), f32[4,64,512]{2,1,0:T(8,128)}) %all-reduce.2.cloned.1.call-update) | async-done | bytes 524304 | tf_op jit(solution)/shard_map/psum | solution.py:99
  65.0 5.1 %collective-permute-start = (bf16[4,64,480]{2,1,0:T(8,128)(2,1)S(1)}, bf16[4,64,480]{2,1,0:T(8,128)(2,1)S(1)}, u32[]{:S(2)}, u32[]{:S(2)}) collective-permute-start(bf16[4,64,480]{2,1,0:T(8,128)(2,1)S(1)} %fusion.1), channel_id=1, source_target_pairs={{0,4},{4,8},{8,12},{12,16},{16,20},{20,24},{24,28},{28,32},{32,36}... | collective-permute-start | bytes 737288 | tf_op jit(solution)/shard_map/ppermute | solution.py:18
  72.0 6.7 %collective-permute-done = bf16[4,64,480]{2,1,0:T(8,128)(2,1)S(1)} collective-permute-done((bf16[4,64,480]{2,1,0:T(8,128)(2,1)S(1)}, bf16[4,64,480]{2,1,0:T(8,128)(2,1)S(1)}, u32[]{:S(2)}, u32[]{:S(2)}) %collective-permute-start) | collective-permute-done | bytes 245792 | tf_op jit(solution)/shard_map/ppermute | solution.py:18
  78.8 4.0 collective-permute-done.1
  86.5 28.4 %all-gather.4.cloned.1.call-done = bf16[128,4,120,120]{3,2,1,0:T(8,128)(2,1)} async-done(((bf16[2,4,120,120]{3,2,1,0:T(8,128)(2,1)}), bf16[128,4,120,120]{3,2,1,0:T(8,128)(2,1)}) %all-gather.4.cloned.1.call-update) | async-done | bytes 14745616 | tf_op jit(solution)/shard_map/all_gather | solution.py:120
  114.9 222.5 %while.16 = (s32[]{:T(128)}, f32[4,64,4,120]{3,1,0,2:T(8,128)}, bf16[128,4,120,120]{3,2,1,0:T(8,128)(2,1)}, bf16[4,192,4,120]{3,1,0,2:T(8,128)(2,1)S(1)}, s32[]{...) while((s32[]{:T(128)}, f32[4,64,4,120]{3,1,0,2:T(8,128)}, ...), condition=%wide.region_5.6_spmd.clone, body=%wide.region_4.5_spmd.clone.sunk | while | flops 472105024 | bytes 34530440 | solution.py:75
  117.9 7.1 %concatenate.26 = bf16[4,64,4,1920]{3,1,0,2:T(8,128)(2,1)} concatenate(bf16[4,64,4,120]{3,1,0,2:T(8,128)(2,1)} %get-tuple-element.238, bf16[4,64,4,120]{3,1,0,2:T(8,128)(2,1)} %get-tuple-element.239, bf16[4,64,4,120]{3,1,0,2:T(8,128)(2,1)} %get-tuple-element.240, bf16[4,64,4,120]{3,1,0,2:T(8,128)(2,1)} %get-tuple-element.241, bf16[4,64,4,120]{3,1,0,2:T(8,128)(2,1)} %get-tuple-element.242, ...), dimensions={3} | concatenate | bytes 7864320 | tf_op jit(solution)/shard_map/while/body/eval_jaxpr/concatenate | solution.py:68
  128.0 4.4 copy.47
  132.5 4.6 reshape.312
  137.1 3.8 fusion.188
  144.8 7.1 %concatenate.26 = bf16[4,64,4,1920]{3,1,0,2:T(8,128)(2,1)} concatenate(bf16[4,64,4,120]{3,1,0,2:T(8,128)(2,1)} %get-tuple-element.238, bf16[4,64,4,120]{3,1,0,2:T(8,128)(2,1)} %get-tuple-element.239, bf16[4,64,4,120]{3,1,0,2:T(8,128)(2,1)} %get-tuple-element.240, bf16[4,64,4,120]{3,1,0,2:T(8,128)(2,1)} %get-tuple-element.241, bf16[4,64,4,120]{3,1,0,2:T(8,128)(2,1)} %get-tuple-element.242, ...), dimensions={3} | concatenate | bytes 7864320 | tf_op jit(solution)/shard_map/while/body/eval_jaxpr/concatenate | solution.py:68
  151.9 3.0 constant_dynamic-slice_fusion.19
  154.9 4.4 copy.47
  159.4 4.6 reshape.312
  164.0 3.8 fusion.188
  172.7 7.1 %concatenate.26 = bf16[4,64,4,1920]{3,1,0,2:T(8,128)(2,1)} concatenate(bf16[4,64,4,120]{3,1,0,2:T(8,128)(2,1)} %get-tuple-element.238, bf16[4,64,4,120]{3,1,0,2:T(8,128)(2,1)} %get-tuple-element.239, bf16[4,64,4,120]{3,1,0,2:T(8,128)(2,1)} %get-tuple-element.240, bf16[4,64,4,120]{3,1,0,2:T(8,128)(2,1)} %get-tuple-element.241, bf16[4,64,4,120]{3,1,0,2:T(8,128)(2,1)} %get-tuple-element.242, ...), dimensions={3} | concatenate | bytes 7864320 | tf_op jit(solution)/shard_map/while/body/eval_jaxpr/concatenate | solution.py:68
  182.9 4.4 copy.47
  187.3 4.6 reshape.312
  191.9 3.8 fusion.188
  200.7 7.1 %concatenate.26 = bf16[4,64,4,1920]{3,1,0,2:T(8,128)(2,1)} concatenate(bf16[4,64,4,120]{3,1,0,2:T(8,128)(2,1)} %get-tuple-element.238, bf16[4,64,4,120]{3,1,0,2:T(8,128)(2,1)} %get-tuple-element.239, bf16[4,64,4,120]{3,1,0,2:T(8,128)(2,1)} %get-tuple-element.240, bf16[4,64,4,120]{3,1,0,2:T(8,128)(2,1)} %get-tuple-element.241, bf16[4,64,4,120]{3,1,0,2:T(8,128)(2,1)} %get-tuple-element.242, ...), dimensions={3} | concatenate | bytes 7864320 | tf_op jit(solution)/shard_map/while/body/eval_jaxpr/concatenate | solution.py:68
  207.8 3.0 constant_dynamic-slice_fusion.19
  210.9 4.4 copy.47
  215.3 4.6 reshape.312
  219.9 3.8 fusion.188
  228.6 7.1 %concatenate.26 = bf16[4,64,4,1920]{3,1,0,2:T(8,128)(2,1)} concatenate(bf16[4,64,4,120]{3,1,0,2:T(8,128)(2,1)} %get-tuple-element.238, bf16[4,64,4,120]{3,1,0,2:T(8,128)(2,1)} %get-tuple-element.239, bf16[4,64,4,120]{3,1,0,2:T(8,128)(2,1)} %get-tuple-element.240, bf16[4,64,4,120]{3,1,0,2:T(8,128)(2,1)} %get-tuple-element.241, bf16[4,64,4,120]{3,1,0,2:T(8,128)(2,1)} %get-tuple-element.242, ...), dimensions={3} | concatenate | bytes 7864320 | tf_op jit(solution)/shard_map/while/body/eval_jaxpr/concatenate | solution.py:68
  238.8 4.4 copy.47
  243.2 4.6 reshape.312
  247.8 3.8 fusion.188
  256.5 7.1 %concatenate.26 = bf16[4,64,4,1920]{3,1,0,2:T(8,128)(2,1)} concatenate(bf16[4,64,4,120]{3,1,0,2:T(8,128)(2,1)} %get-tuple-element.238, bf16[4,64,4,120]{3,1,0,2:T(8,128)(2,1)} %get-tuple-element.239, bf16[4,64,4,120]{3,1,0,2:T(8,128)(2,1)} %get-tuple-element.240, bf16[4,64,4,120]{3,1,0,2:T(8,128)(2,1)} %get-tuple-element.241, bf16[4,64,4,120]{3,1,0,2:T(8,128)(2,1)} %get-tuple-element.242, ...), dimensions={3} | concatenate | bytes 7864320 | tf_op jit(solution)/shard_map/while/body/eval_jaxpr/concatenate | solution.py:68
  263.7 3.0 constant_dynamic-slice_fusion.19
  266.7 4.4 copy.47
  271.2 4.6 reshape.312
  275.7 3.8 fusion.188
  284.5 7.1 %concatenate.26 = bf16[4,64,4,1920]{3,1,0,2:T(8,128)(2,1)} concatenate(bf16[4,64,4,120]{3,1,0,2:T(8,128)(2,1)} %get-tuple-element.238, bf16[4,64,4,120]{3,1,0,2:T(8,128)(2,1)} %get-tuple-element.239, bf16[4,64,4,120]{3,1,0,2:T(8,128)(2,1)} %get-tuple-element.240, bf16[4,64,4,120]{3,1,0,2:T(8,128)(2,1)} %get-tuple-element.241, bf16[4,64,4,120]{3,1,0,2:T(8,128)(2,1)} %get-tuple-element.242, ...), dimensions={3} | concatenate | bytes 7864320 | tf_op jit(solution)/shard_map/while/body/eval_jaxpr/concatenate | solution.py:68
  291.6 3.0 constant_dynamic-slice_fusion.19
  294.7 4.4 copy.47
  299.1 4.6 reshape.312
  303.7 3.9 fusion.188
  312.5 7.1 %concatenate.26 = bf16[4,64,4,1920]{3,1,0,2:T(8,128)(2,1)} concatenate(bf16[4,64,4,120]{3,1,0,2:T(8,128)(2,1)} %get-tuple-element.238, bf16[4,64,4,120]{3,1,0,2:T(8,128)(2,1)} %get-tuple-element.239, bf16[4,64,4,120]{3,1,0,2:T(8,128)(2,1)} %get-tuple-element.240, bf16[4,64,4,120]{3,1,0,2:T(8,128)(2,1)} %get-tuple-element.241, bf16[4,64,4,120]{3,1,0,2:T(8,128)(2,1)} %get-tuple-element.242, ...), dimensions={3} | concatenate | bytes 7864320 | tf_op jit(solution)/shard_map/while/body/eval_jaxpr/concatenate | solution.py:68
  319.6 3.0 constant_dynamic-slice_fusion.19
  322.7 4.4 copy.47
  327.1 4.6 reshape.312
  331.7 3.8 fusion.188
  340.7 3.8 fusion.4
  347.1 19.4 %reduce-scatter.2.cloned.1.call-done = f32[1,64,1024]{2,1,0:T(8,128)} async-done(((f32[4,64,1024]{2,1,0:T(8,128)}), f32[1,64,1024]{2,1,0:T(8,128)}) %reduce-scatter.2.cloned.1.call-update) | async-done | bytes 262160 | tf_op jit(solution)/shard_map/reduce_scatter | solution.py:127
  369.3 41.1 %all-gather.6.cloned.1.call-done = bf16[1024,1024]{1,0:T(8,128)(2,1)} async-done(((bf16[64,1024]{1,0:T(8,128)(2,1)}), bf16[1024,1024]{1,0:T(8,128)(2,1)}) %all-gather.6.cloned.1.call-update) | async-done | bytes 2097168 | tf_op jit(solution)/shard_map/all_gather | solution.py:134
  412.7 48.5 %gather_fusion = f32[6400]{0:T(1024)S(1)} fusion(f32[1,64,1024]{2,1,0:T(8,128)S(1)} %convolution_bitcast_fusion, s32[6400]{0:T(1024)S(1)} %reshape.273), kind=kCustom, calls=%fused_computation | custom fusion | bytes 128000 | tf_op jit(solution)/shard_map/vmap(jit(take_along_axis))/gather | solution.py:47
  463.3 35.1 %gather_fusion.1 = f32[6400]{0:T(1024)S(1)} fusion(f32[1,1024]{1,0:T(1,128)S(1)} %bitcast.82, s32[6400]{0:T(1024)S(1)} %reshape.281), kind=kCustom, calls=%fused_computation.1 | custom fusion | bytes 102400 | tf_op jit(solution)/shard_map/vmap()/gather | solution.py:48
  (78 shorter events, 75.8 us)
Async XLA Ops:
  7.4 359.2 %copy-start = (bf16[1024,1024]{1,0:T(8,128)(2,1)S(1)}, bf16[1024,1024]{1,0:T(8,128)(2,1)}, u32[]{:S(2)}) copy-start(bf16[1024,1024]{1,0:T(8,128)(2,1)} %param.20) | copy-start | bytes 6291460
  7.4 53.8 %all-reduce.2.cloned.1.call-start = ((), (), s32[]{:S(2)}) async-start(), calls=%async_computation.1 | async-start | bytes 1048576 | tf_op jit(solution)/shard_map/psum | solution.py:99
  10.5 104.4 %all-gather.4.cloned.1.call-start = ((), (), s32[]{:S(2)}) async-start(), calls=%async_computation.2 | async-start | bytes 15974400 | tf_op jit(solution)/shard_map/all_gather | solution.py:120
  11.1 355.5 %reduce-scatter.2.cloned.1.call-start = ((), (), s32[]{:S(2)}) async-start(), calls=%async_computation.3 | async-start | bytes 1310720 | tf_op jit(solution)/shard_map/reduce_scatter | solution.py:127
  65.0 49.9 %copy-start.2 = (bf16[4,64,480]{2,1,0:T(8,128)(2,1)}, bf16[4,64,480]{2,1,0:T(8,128)(2,1)S(1)}, u32[]{:S(2)}) copy-start(bf16[4,64,480]{2,1,0:T(8,128)(2,1)S(1)} %fusion.1) | copy-start | bytes 737284
  65.0 13.7 %collective-permute-start = (bf16[4,64,480]{2,1,0:T(8,128)(2,1)S(1)}, bf16[4,64,480]{2,1,0:T(8,128)(2,1)S(1)}, u32[]{:S(2)}, u32[]{:S(2)}) collective-permute-start(bf16[4,64,480]{2,1,0:T(8,128)(2,1)S(1)} %fusion.1), channel_id=1, source_target_pairs={{0,4},{4,8},{8,12},{12,16},{16,20},{20,24},{24,28},{28,32},{32,36}... | collective-permute-start | bytes 737288 | tf_op jit(solution)/shard_map/ppermute | solution.py:18
  70.1 12.7 %collective-permute-start.1 = (bf16[4,64,480]{2,1,0:T(8,128)(2,1)S(1)}, bf16[4,64,480]{2,1,0:T(8,128)(2,1)}, u32[]{:S(2)}, u32[]{:S(2)}) collective-permute-start(bf16[4,64,480]{2,1,0:T(8,128)(2,1)S(1)} %fusion.1), channel_id=1, source_target_pairs={{4,0},{8,4},{12,8},{16,12},{20,16},{24,20},{28,24},{32,28},{36,32}... | collective-permute-start | bytes 737288 | tf_op jit(solution)/shard_map/ppermute | solution.py:21
  337.5 3.2 copy-start.3
  340.7 4.1 copy-start.5
  344.5 24.4 %copy-start.4 = (s32[1,64,100]{2,1,0:T(8,128)S(1)}, s32[1,64,100]{2,1,0:T(8,128)}, u32[]{:S(2)}) copy-start(s32[1,64,100]{2,1,0:T(8,128)} %param.23) | copy-start | bytes 76804
  344.5 65.8 %all-gather.6.cloned.1.call-start = ((), (), s32[]{:S(2)}) async-start(), calls=%async_computation.4 | async-start | bytes 2228224 | tf_op jit(solution)/shard_map/all_gather | solution.py:134
  366.5 43.8 %copy-start.1 = (f32[1,64,1024]{2,1,0:T(8,128)S(1)}, f32[1,64,1024]{2,1,0:T(8,128)}, u32[]{:S(2)}) copy-start(f32[1,64,1024]{2,1,0:T(8,128)} %reduce-scatter.2.cloned.1.call-done) | copy-start | bytes 786436
Sparse Core Ops, SparseCore 0:
  10.6 50.5 all-reduce.1
  344.6 21.8 reduce-scatter.1
  369.0 41.2 all-gather.5
Sparse Core Ops, SparseCore 1:
  13.7 101.2 all-gather.3
where the time goes:
time: 514 us; the launch traced here: 506 us
  local copies, waits for them, and re-layouts  267 us (52%)
  waiting for transfers between devices  149 us (29%)
  matrix products  46.2 us (9%)
  other arithmetic  22.3 us (4%)
  between operations  14.8 us (3%)
  starting transfers between devices  7.3 us (1%)
    dynamic_slice x16, local copies, waits for them, and re-layouts, add_block(): taps = lax.dynamic_slice_in_dim(tap_block, base, joined_taps, 0)  59.7 us
    concatenate x8, local copies, waits for them, and re-layouts, add_block(): joined = jnp.concatenate(slabs, axis=-1)  57.2 us
    gather x4, local copies, waits for them, and re-layouts, utterance_loss(): neg_dot = jnp.take_along_axis(scores, neg_ids, axis=1)  48.7 us
    psum x1, waiting for transfers between devices, on_device(): summed = lax.psum(conv_term, 'tensor')  48.5 us
    all_gather x1, waiting for transfers between devices, on_device(): all_targets = lax.all_gather(own_targets, 'seq', axis=1, tiled=True)  41.1 us
    reshape x8, local copies, waits for them, and re-layouts, add_block(): jnp.transpose(taps, (1, 0, 2, 3))  36.6 us
    gather x3, local copies, waits for them, and re-layouts, utterance_loss(): neg_norm = tgt_norm[neg_ids]  35.2 us
    while x8, matrix products  30.8 us
  transfers between devices with their start and end apart: 6, of which 6 were waited for; matrix products, arithmetic and copies ran while one was open for 2% of the time, Pallas kernels for 0%

commit v1 on v0

--- a/solution.py
+++ b/solution.py
@@ -96,7 +96,7 @@
         conv_weight.reshape(2 * channels, conv_weight.shape[2]),
         preferred_element_type=jnp.float32,
     )
-    summed = lax.psum(conv_term, "tensor")
+    summed = jnp.sum(lax.all_gather(conv_term, axis_name="tensor"), 0)
     row_mean = jnp.mean(summed, axis=-1, keepdims=True)
     row_square = jnp.mean(summed * summed, axis=-1, keepdims=True)
     normed = (summed - row_mean) * lax.rsqrt(row_square - row_mean * row_mean + ln_eps)

time: 514 us -> 545 us (1.060)
  waiting for transfers between devices: 149 us -> 180 us
    all_gather x1, waiting for transfers between devices: 28.4 us -> 78.8 us  [on_device(): lax.all_gather(pos_weight, ('dp', 'seq'), axis=0, tiled=True)]
    psum x1 -> x0, waiting for transfers between devices: 48.5 us -> none  [on_device(): summed = lax.psum(conv_term, 'tensor')]
    all_gather x0 -> x1, waiting for transfers between devices: none -> 35 us  [on_device(): summed = jnp.sum(lax.all_gather(conv_term, axis_name='tensor'), 0)]
  transfers between devices with their start and end apart: 6 -> 6, of which waited for: 6 -> 6; matrix products, arithmetic and copies ran while one was open for 2% -> 3% of each run, Pallas kernels for 0% -> 0%
where the time goes in v1:
time: 545 us; the launch traced here: 538 us
  local copies, waits for them, and re-layouts  267 us (49%)
  waiting for transfers between devices  180 us (33%)
  matrix products  46 us (8%)
  other arithmetic  24.9 us (5%)
  between operations  13.4 us (2%)
  starting transfers between devices  5.96 us (1%)
    all_gather x1, waiting for transfers between devices, on_device(): lax.all_gather(pos_weight, ('dp', 'seq'), axis=0, tiled=True)  78.8 us
    dynamic_slice x16, local copies, waits for them, and re-layouts, add_block(): taps = lax.dynamic_slice_in_dim(tap_block, base, joined_taps, 0)  59.7 us
    concatenate x8, local copies, waits for them, and re-layouts, add_block(): joined = jnp.concatenate(slabs, axis=-1)  57.2 us
    gather x4, local copies, waits for them, and re-layouts, utterance_loss(): neg_dot = jnp.take_along_axis(scores, neg_ids, axis=1)  48.7 us
    all_gather x1, waiting for transfers between devices, on_device(): all_targets = lax.all_gather(own_targets, 'seq', axis=1, tiled=True)  41 us
    reshape x8, local copies, waits for them, and re-layouts, add_block(): jnp.transpose(taps, (1, 0, 2, 3))  36.6 us
    gather x3, local copies, waits for them, and re-layouts, utterance_loss(): neg_norm = tgt_norm[neg_ids]  35.2 us
    all_gather x1, waiting for transfers between devices, on_device(): summed = jnp.sum(lax.all_gather(conv_term, axis_name='tensor'), 0)  35 us
  transfers between devices with their start and end apart: 6, of which 6 were waited for; matrix products, arithmetic and copies ran while one was open for 3% of the time, Pallas kernels for 0%

profile of v1, /device:TPU:1, one launch (start us, length us, event | category | flops | bytes accessed | tf_op | source)
XLA Modules:
  0.0 537.7 jit_solution(7318156916189150504)
XLA Ops:
  12.1 35.0 %all-gather.8.cloned.1.call-done = f32[16,64,512]{2,1,0:T(8,128)} async-done(((f32[4,64,512]{2,1,0:T(8,128)}), f32[16,64,512]{2,1,0:T(8,128)}) %all-gather.8.cloned.1.call-update) | async-done | bytes 2097168 | tf_op jit(solution)/shard_map/all_gather | solution.py:99
  53.3 3.7 collective-permute-start
  60.4 4.5 collective-permute-done.1
  68.6 78.8 %all-gather.6.cloned.1.call-done = bf16[128,4,120,120]{3,2,1,0:T(8,128)(2,1)} async-done(((bf16[2,4,120,120]{3,2,1,0:T(8,128)(2,1)}), bf16[128,4,120,120]{3,2,1,0:T(8,128)(2,1)}) %all-gather.6.cloned.1.call-update) | async-done | bytes 14745616 | tf_op jit(solution)/shard_map/all_gather | solution.py:120
  147.4 222.5 %while.16 = (s32[]{:T(128)}, f32[4,64,4,120]{3,1,0,2:T(8,128)}, bf16[128,4,120,120]{3,2,1,0:T(8,128)(2,1)}, bf16[4,192,4,120]{3,1,0,2:T(8,128)(2,1)S(1)}, s32[]{...) while((s32[]{:T(128)}, f32[4,64,4,120]{3,1,0,2:T(8,128)}, ...), condition=%wide.region_5.6_spmd.clone, body=%wide.region_4.5_spmd.clone.sunk | while | flops 472105024 | bytes 34530440 | solution.py:75
  150.4 7.1 %concatenate.26 = bf16[4,64,4,1920]{3,1,0,2:T(8,128)(2,1)} concatenate(bf16[4,64,4,120]{3,1,0,2:T(8,128)(2,1)} %get-tuple-element.236, bf16[4,64,4,120]{3,1,0,2:T(8,128)(2,1)} %get-tuple-element.237, bf16[4,64,4,120]{3,1,0,2:T(8,128)(2,1)} %get-tuple-element.238, bf16[4,64,4,120]{3,1,0,2:T(8,128)(2,1)} %get-tuple-element.239, bf16[4,64,4,120]{3,1,0,2:T(8,128)(2,1)} %get-tuple-element.240, ...), dimensions={3} | concatenate | bytes 7864320 | tf_op jit(solution)/shard_map/while/body/eval_jaxpr/concatenate | solution.py:68
  157.5 3.0 constant_dynamic-slice_fusion.19
  160.6 4.4 copy.47
  165.0 4.6 reshape.314
  169.6 3.8 fusion.187
  177.3 7.1 %concatenate.26 = bf16[4,64,4,1920]{3,1,0,2:T(8,128)(2,1)} concatenate(bf16[4,64,4,120]{3,1,0,2:T(8,128)(2,1)} %get-tuple-element.236, bf16[4,64,4,120]{3,1,0,2:T(8,128)(2,1)} %get-tuple-element.237, bf16[4,64,4,120]{3,1,0,2:T(8,128)(2,1)} %get-tuple-element.238, bf16[4,64,4,120]{3,1,0,2:T(8,128)(2,1)} %get-tuple-element.239, bf16[4,64,4,120]{3,1,0,2:T(8,128)(2,1)} %get-tuple-element.240, ...), dimensions={3} | concatenate | bytes 7864320 | tf_op jit(solution)/shard_map/while/body/eval_jaxpr/concatenate | solution.py:68
  184.5 3.0 constant_dynamic-slice_fusion.19
  187.5 4.4 copy.47
  191.9 4.6 reshape.314
  196.5 3.8 fusion.187
  205.2 7.1 %concatenate.26 = bf16[4,64,4,1920]{3,1,0,2:T(8,128)(2,1)} concatenate(bf16[4,64,4,120]{3,1,0,2:T(8,128)(2,1)} %get-tuple-element.236, bf16[4,64,4,120]{3,1,0,2:T(8,128)(2,1)} %get-tuple-element.237, bf16[4,64,4,120]{3,1,0,2:T(8,128)(2,1)} %get-tuple-element.238, bf16[4,64,4,120]{3,1,0,2:T(8,128)(2,1)} %get-tuple-element.239, bf16[4,64,4,120]{3,1,0,2:T(8,128)(2,1)} %get-tuple-element.240, ...), dimensions={3} | concatenate | bytes 7864320 | tf_op jit(solution)/shard_map/while/body/eval_jaxpr/concatenate | solution.py:68
  212.4 3.0 constant_dynamic-slice_fusion.19
  215.4 4.4 copy.47
  219.9 4.6 reshape.314
  224.4 3.8 fusion.187
  233.2 7.1 %concatenate.26 = bf16[4,64,4,1920]{3,1,0,2:T(8,128)(2,1)} concatenate(bf16[4,64,4,120]{3,1,0,2:T(8,128)(2,1)} %get-tuple-element.236, bf16[4,64,4,120]{3,1,0,2:T(8,128)(2,1)} %get-tuple-element.237, bf16[4,64,4,120]{3,1,0,2:T(8,128)(2,1)} %get-tuple-element.238, bf16[4,64,4,120]{3,1,0,2:T(8,128)(2,1)} %get-tuple-element.239, bf16[4,64,4,120]{3,1,0,2:T(8,128)(2,1)} %get-tuple-element.240, ...), dimensions={3} | concatenate | bytes 7864320 | tf_op jit(solution)/shard_map/while/body/eval_jaxpr/concatenate | solution.py:68
  240.4 3.0 constant_dynamic-slice_fusion.19
  243.4 4.4 copy.47
  247.8 4.6 reshape.314
  252.4 3.8 fusion.187
  261.1 7.1 %concatenate.26 = bf16[4,64,4,1920]{3,1,0,2:T(8,128)(2,1)} concatenate(bf16[4,64,4,120]{3,1,0,2:T(8,128)(2,1)} %get-tuple-element.236, bf16[4,64,4,120]{3,1,0,2:T(8,128)(2,1)} %get-tuple-element.237, bf16[4,64,4,120]{3,1,0,2:T(8,128)(2,1)} %get-tuple-element.238, bf16[4,64,4,120]{3,1,0,2:T(8,128)(2,1)} %get-tuple-element.239, bf16[4,64,4,120]{3,1,0,2:T(8,128)(2,1)} %get-tuple-element.240, ...), dimensions={3} | concatenate | bytes 7864320 | tf_op jit(solution)/shard_map/while/body/eval_jaxpr/concatenate | solution.py:68
  268.3 3.0 constant_dynamic-slice_fusion.19
  271.3 4.4 copy.47
  275.7 4.6 reshape.314
  280.3 3.8 fusion.187
  289.1 7.1 %concatenate.26 = bf16[4,64,4,1920]{3,1,0,2:T(8,128)(2,1)} concatenate(bf16[4,64,4,120]{3,1,0,2:T(8,128)(2,1)} %get-tuple-element.236, bf16[4,64,4,120]{3,1,0,2:T(8,128)(2,1)} %get-tuple-element.237, bf16[4,64,4,120]{3,1,0,2:T(8,128)(2,1)} %get-tuple-element.238, bf16[4,64,4,120]{3,1,0,2:T(8,128)(2,1)} %get-tuple-element.239, bf16[4,64,4,120]{3,1,0,2:T(8,128)(2,1)} %get-tuple-element.240, ...), dimensions={3} | concatenate | bytes 7864320 | tf_op jit(solution)/shard_map/while/body/eval_jaxpr/concatenate | solution.py:68
  296.2 3.0 constant_dynamic-slice_fusion.19
  299.2 4.4 copy.47
  303.7 4.6 reshape.314
  308.3 3.8 fusion.187
  317.0 7.1 %concatenate.26 = bf16[4,64,4,1920]{3,1,0,2:T(8,128)(2,1)} concatenate(bf16[4,64,4,120]{3,1,0,2:T(8,128)(2,1)} %get-tuple-element.236, bf16[4,64,4,120]{3,1,0,2:T(8,128)(2,1)} %get-tuple-element.237, bf16[4,64,4,120]{3,1,0,2:T(8,128)(2,1)} %get-tuple-element.238, bf16[4,64,4,120]{3,1,0,2:T(8,128)(2,1)} %get-tuple-element.239, bf16[4,64,4,120]{3,1,0,2:T(8,128)(2,1)} %get-tuple-element.240, ...), dimensions={3} | concatenate | bytes 7864320 | tf_op jit(solution)/shard_map/while/body/eval_jaxpr/concatenate | solution.py:68
  327.2 4.4 copy.47
  331.6 4.6 reshape.314
  336.2 3.8 fusion.187
  345.0 7.1 %concatenate.26 = bf16[4,64,4,1920]{3,1,0,2:T(8,128)(2,1)} concatenate(bf16[4,64,4,120]{3,1,0,2:T(8,128)(2,1)} %get-tuple-element.236, bf16[4,64,4,120]{3,1,0,2:T(8,128)(2,1)} %get-tuple-element.237, bf16[4,64,4,120]{3,1,0,2:T(8,128)(2,1)} %get-tuple-element.238, bf16[4,64,4,120]{3,1,0,2:T(8,128)(2,1)} %get-tuple-element.239, bf16[4,64,4,120]{3,1,0,2:T(8,128)(2,1)} %get-tuple-element.240, ...), dimensions={3} | concatenate | bytes 7864320 | tf_op jit(solution)/shard_map/while/body/eval_jaxpr/concatenate | solution.py:68
  355.2 4.4 copy.47
  359.6 4.6 reshape.314
  364.2 3.8 fusion.187
  373.2 3.8 fusion.4
  379.6 18.8 %reduce-scatter.2.cloned.1.call-done = f32[1,64,1024]{2,1,0:T(8,128)} async-done(((f32[4,64,1024]{2,1,0:T(8,128)}), f32[1,64,1024]{2,1,0:T(8,128)}) %reduce-scatter.2.cloned.1.call-update) | async-done | bytes 262160 | tf_op jit(solution)/shard_map/reduce_scatter | solution.py:127
  401.2 41.0 %all-gather.10.cloned.1.call-done = bf16[1024,1024]{1,0:T(8,128)(2,1)} async-done(((bf16[64,1024]{1,0:T(8,128)(2,1)}), bf16[1024,1024]{1,0:T(8,128)(2,1)}) %all-gather.10.cloned.1.call-update) | async-done | bytes 2097168 | tf_op jit(solution)/shard_map/all_gather | solution.py:134
  444.6 48.5 %gather_fusion = f32[6400]{0:T(1024)S(1)} fusion(f32[1,64,1024]{2,1,0:T(8,128)S(1)} %convolution_bitcast_fusion, s32[6400]{0:T(1024)S(1)} %reshape.273), kind=kCustom, calls=%fused_computation | custom fusion | bytes 128000 | tf_op jit(solution)/shard_map/vmap(jit(take_along_axis))/gather | solution.py:47
  495.3 35.1 %gather_fusion.1 = f32[6400]{0:T(1024)S(1)} fusion(f32[1,1024]{1,0:T(1,128)S(1)} %bitcast.84, s32[6400]{0:T(1024)S(1)} %reshape.281), kind=kCustom, calls=%fused_computation.1 | custom fusion | bytes 102400 | tf_op jit(solution)/shard_map/vmap()/gather | solution.py:48
  (83 shorter events, 76.7 us)
Async XLA Ops:
  6.5 391.9 %copy-start = (bf16[1024,1024]{1,0:T(8,128)(2,1)S(1)}, bf16[1024,1024]{1,0:T(8,128)(2,1)}, u32[]{:S(2)}) copy-start(bf16[1024,1024]{1,0:T(8,128)(2,1)} %param.20) | copy-start | bytes 6291460
  6.5 40.5 %all-gather.8.cloned.1.call-start = ((), (), s32[]{:S(2)}) async-start(), calls=%async_computation.3 | async-start | bytes 2621440 | tf_op jit(solution)/shard_map/all_gather | solution.py:99
  7.6 43.2 %copy-start.6 = (bf16[480]{0:T(512)(128)(2,1)S(1)}, bf16[480]{0:T(512)(128)(2,1)}, u32[]{:S(2)}) copy-start(bf16[480]{0:T(512)(128)(2,1)} %param.16) | copy-start | bytes 2884
  9.7 137.8 %all-gather.6.cloned.1.call-start = ((), (), s32[]{:S(2)}) async-start(), calls=%async_computation.1 | async-start | bytes 15974400 | tf_op jit(solution)/shard_map/all_gather | solution.py:120
  10.4 388.0 %reduce-scatter.2.cloned.1.call-start = ((), (), s32[]{:S(2)}) async-start(), calls=%async_computation.2 | async-start | bytes 1310720 | tf_op jit(solution)/shard_map/reduce_scatter | solution.py:127
  53.3 94.1 %copy-start.2 = (bf16[4,64,480]{2,1,0:T(8,128)(2,1)}, bf16[4,64,480]{2,1,0:T(8,128)(2,1)S(1)}, u32[]{:S(2)}) copy-start(bf16[4,64,480]{2,1,0:T(8,128)(2,1)S(1)} %fusion.1) | copy-start | bytes 737284
  53.3 7.0 %collective-permute-start = (bf16[4,64,480]{2,1,0:T(8,128)(2,1)S(1)}, bf16[4,64,480]{2,1,0:T(8,128)(2,1)S(1)}, u32[]{:S(2)}, u32[]{:S(2)}) collective-permute-start(bf16[4,64,480]{2,1,0:T(8,128)(2,1)S(1)} %fusion.1), channel_id=1, source_target_pairs={{0,4},{4,8},{8,12},{12,16},{16,20},{20,24},{24,28},{28,32},{32,36}... | collective-permute-start | bytes 737288 | tf_op jit(solution)/shard_map/ppermute | solution.py:18
  57.1 7.8 %collective-permute-start.1 = (bf16[4,64,480]{2,1,0:T(8,128)(2,1)S(1)}, bf16[4,64,480]{2,1,0:T(8,128)(2,1)}, u32[]{:S(2)}, u32[]{:S(2)}) collective-permute-start(bf16[4,64,480]{2,1,0:T(8,128)(2,1)S(1)} %fusion.1), channel_id=1, source_target_pairs={{4,0},{8,4},{12,8},{16,12},{20,16},{24,20},{28,24},{32,28},{36,32}... | collective-permute-start | bytes 737288 | tf_op jit(solution)/shard_map/ppermute | solution.py:21
  369.9 3.2 copy-start.3
  373.2 4.1 copy-start.5
  377.0 23.9 %copy-start.4 = (s32[1,64,100]{2,1,0:T(8,128)S(1)}, s32[1,64,100]{2,1,0:T(8,128)}, u32[]{:S(2)}) copy-start(s32[1,64,100]{2,1,0:T(8,128)} %param.23) | copy-start | bytes 76804
  377.0 65.3 %all-gather.10.cloned.1.call-start = ((), (), s32[]{:S(2)}) async-start(), calls=%async_computation.4 | async-start | bytes 2228224 | tf_op jit(solution)/shard_map/all_gather | solution.py:134
  398.5 43.8 %copy-start.1 = (f32[1,64,1024]{2,1,0:T(8,128)S(1)}, f32[1,64,1024]{2,1,0:T(8,128)}, u32[]{:S(2)}) copy-start(f32[1,64,1024]{2,1,0:T(8,128)} %reduce-scatter.2.cloned.1.call-done) | copy-start | bytes 786436
Sparse Core Ops, SparseCore 0:
  9.8 37.2 all-gather.7
  49.8 97.5 all-gather.5
  377.1 21.3 reduce-scatter.1
  400.9 41.2 all-gather.9
